TPU v7x, 32 devices: a whole 2x2x4 slice. The times are simulated.
32 devices in a mesh: group: 2 (over y), swap: 8 (over z, x), image: 2 (over core).
Axes of the slice: x: 2, y: 2, z: 4, core: 2. Of those that a mesh axis runs over, the one named last changes fastest.
Arguments:
- images_in: bfloat16 [16, 1536, 4096], P(('group', 'image'), 'swap'), parts along dimension 0, may hold values from -6 to 6
- kernel: bfloat16 [1536, 49], P('swap'), may hold values from -1.75 to 1.75
- conv_bias: float32 [1536], P('swap'), may hold values from -1 to 1
- norm_gain: float32 [1536], replicated, may hold values from 0.1 to 1.9
- norm_shift: float32 [1536], replicated, may hold values from -0.5 to 0.5
- fp8_weight: bfloat16 [1536, 6144], P('swap', 'image'), may hold values from -1.875 to 1.875, as said below
- block_scale: int32 [1536, 48], P('swap', 'image'), may hold values from -7 to -5
- adapter_a: bfloat16 [1536, 32], replicated, may hold values from -0.15625 to 0.15625
- adapter_b: bfloat16 [32, 6144], P(None, 'image'), may hold values from -0.25 to 0.25
- cotangent: bfloat16 [16, 4096, 6144], P('group', 'swap', 'image'), parts along dimension 0, may hold values from -0.05 to 0.05
Outputs:
- grad_a: float32 [3072, 32], P('group'), parts along dimension 0
- grad_b: float32 [64, 6144], P('group', 'image'), parts along dimension 0
There are 2 independent parts, one for each index of `group`. A program takes and returns all parts, laid end to end along the dimension named above; an argument that names none is the same for every part. Nothing has to cross between parts.
Inputs may be any that keep to these rules, and one draw needn't show every extreme that they name: `fp8_weight`: each entry is a value of the E4M3 format: a sign times 2 to an integer power times 1 + k / 8 for an integer k of 0 to 7. `block_scale`: the entry at [c, j] is the exponent of the scale of hidden units 128 * j to 128 * j + 127 of weight row c.
All inputs are finite; a program needn't handle non-finite values.
Results may differ from a plain program's by a relative error of at most 0.00055.
The roundings to bfloat16 on the way count: a program that leaves them out, or rounds other values in their place, can miss the bound.
Values may be sent and summed in bfloat16 or wider, within the bound.
A program may use at most 192 MiB of HBM per device.

v0:
```python
import jax
import jax.numpy as jnp
from jax import lax
from jax.sharding import PartitionSpec as P

KS = 7
W = 64
adapter_scale = 2.0
norm_eps = 1e-06


def power_table(scales):
    factor = jnp.zeros(scales.shape, jnp.float32)
    for exponent in range(-12, 4):
        factor = factor + jnp.where(
            scales == exponent, jnp.float32(2.0**exponent), jnp.float32(0.0)
        )
    return factor


def decode(weight, scales):
    row_count = weight.shape[0]
    groups = scales.shape[1]
    blocks = (
        weight.reshape(row_count, groups, -1).astype(jnp.float32) * power_table(scales)[:, :, None]
    )
    return blocks.reshape(row_count, -1).astype(jnp.bfloat16)


def gelu_slope(pre_act):
    cumulative = 0.5 * (1.0 + jax.scipy.special.erf(pre_act * 0.7071067811865476))
    density = jnp.exp(-0.5 * pre_act * pre_act) * 0.3989422804014327
    return cumulative + pre_act * density


def depthwise(images, kernel, conv_bias, map_width):
    batch, channels, pixels = images.shape
    maps = images.reshape(batch, channels, pixels // map_width, map_width)
    taps = kernel.reshape(channels, 1, KS, KS)
    half_span = KS // 2
    summed = lax.conv_general_dilated(
        maps,
        taps,
        (1, 1),
        ((half_span, half_span), (half_span, half_span)),
        dimension_numbers=("NCHW", "OIHW", "NCHW"),
        feature_group_count=channels,
        preferred_element_type=jnp.float32,
    )
    summed = summed.reshape(batch, channels, pixels)
    return summed + conv_bias[None, :, None]


def shards(
    images_in,
    kernel,
    conv_bias,
    norm_gain,
    norm_shift,
    fp8_weight,
    block_scale,
    adapter_a,
    adapter_b,
    cotangent,
):
    conv = depthwise(images_in, kernel, conv_bias, W).astype(jnp.bfloat16)
    values = lax.all_to_all(conv, "swap", split_axis=2, concat_axis=1, tiled=True).astype(
        jnp.float32
    )
    average = jnp.mean(values, axis=1, keepdims=True)
    centred = values - average
    variance = jnp.mean(centred * centred, axis=1, keepdims=True)
    scaled = (
        centred * lax.rsqrt(variance + norm_eps) * norm_gain[None, :, None]
        + norm_shift[None, :, None]
    )
    normed = jnp.swapaxes(scaled, 1, 2).astype(jnp.bfloat16)
    own_rows = normed.reshape(-1, normed.shape[2])
    tokens = lax.all_gather(own_rows, "image", axis=0, tiled=True)
    zero_start = jnp.zeros((tokens.shape[0], fp8_weight.shape[1]), jnp.float32)
    local_weight = decode(fp8_weight, block_scale)
    shard_rows = lax.all_gather(local_weight, "swap", axis=0, tiled=True)
    columns = lax.slice_in_dim(tokens, 0, shard_rows.shape[0], axis=1)
    frozen = zero_start + jnp.dot(columns, shard_rows, preferred_element_type=jnp.float32)
    low_rank = jnp.dot(tokens, adapter_a, preferred_element_type=jnp.float32).astype(jnp.bfloat16)
    pre_act = frozen + adapter_scale * jnp.dot(
        low_rank, adapter_b, preferred_element_type=jnp.float32
    )
    upstream = cotangent.reshape(-1, cotangent.shape[2])
    grad_pre = (upstream.astype(jnp.float32) * gelu_slope(pre_act)).astype(jnp.bfloat16)
    grad_b_local = adapter_scale * jnp.dot(low_rank.T, grad_pre, preferred_element_type=jnp.float32)
    partial_back = jnp.dot(grad_pre, adapter_b.T, preferred_element_type=jnp.float32)
    contract = (((0,), (0,)), ((), ()))
    tokens_wide = tokens.astype(jnp.float32)
    summed_back = lax.psum(partial_back, "image")
    grad_a_local = adapter_scale * lax.dot_general(
        tokens_wide,
        summed_back,
        contract,
        precision=lax.Precision.HIGHEST,
        preferred_element_type=jnp.float32,
    )
    grad_a, grad_b = lax.psum((grad_a_local, grad_b_local), "swap")
    return (grad_a, grad_b)


def solution(mesh):
    placed = (
        P(("group", "image"), "swap", None),
        P("swap", None),
        P("swap"),
        P(),
        P(),
        P("swap", "image"),
        P("swap", "image"),
        P(),
        P(None, "image"),
        P("group", "swap", "image"),
    )
    return jax.shard_map(
        shards,
        mesh=mesh,
        in_specs=placed,
        out_specs=(P("group", None), P("group", "image")),
        check_vma=False,
    )
```

profile of v0, /device:TPU:0, one launch (start us, length us, event | category | flops | bytes accessed | tf_op | source)
XLA Modules:
  0.0 837.5 jit_solution(14557225846373415734)
XLA Ops:
  8.1 10.6 %copy.43 = bf16[4,192,4096]{1,2,0:T(8,128)(2,1)} copy(bf16[4,192,4096]{2,1,0:T(8,128)(2,1)} %param.10) | data formatting | bytes 12582912 | tf_op args[0]
  18.7 11.5 %copy.54 = bf16[192,64,4,64]{0,1,3,2:T(8,128)(2,1)} copy(bf16[192,64,4,64]{0,3,1,2:T(8,128)(2,1)} %bitcast.75) | data formatting | bytes 12582912
  30.2 10.0 %pad.clone = bf16[192,64,4,72]{0,1,3,2:T(8,128)(2,1)} pad(bf16[192,64,4,64]{0,1,3,2:T(8,128)(2,1)} %copy.54, bf16[]{:T(256)} %constant.37), padding=0_0x0_0x0_0x3_5 | pad | bytes 13369346 | tf_op jit(solution)/shard_map/reshape | solution.py:38
  49.7 95.5 %broadcast_select_fusion = f32[64,32,9,192]{3,1,2,0:T(8,128)S(1)} fusion(pred[32,9]{0,1:T(8,128)(4,1)S(1)} %copy-done.9, bf16[192,1,7,7]{0,1,3,2:T(2,128)(2,1)S(1)} %reshape.62, bf16[192,64,4,8,15]{0,1,4,3,2:T(8,128)(2,1)S(1)} %fusion.8), kind=kOutput, calls=%fused_computation.23 | convolution fusion | flops 341065728 | bytes 25971360 | tf_op jit(solution)/shard_map/conv_general_dilated | solution.py:41
  145.3 20.1 %copy.47 = f32[64,32,9,192]{3,0,2,1:T(8,128)S(1)} copy(f32[64,32,9,192]{3,1,2,0:T(8,128)S(1)} %broadcast_select_fusion) | data formatting | bytes 28311552 | tf_op jit(solution)/shard_map/conv_general_dilated | solution.py:41
  167.4 17.9 %copy.48 = f32[4,192,64,64]{1,3,2,0:T(8,128)S(1)} copy(f32[4,192,64,64]{1,2,3,0:T(8,128)S(1)} %slice_bitcast_fusion) | data formatting | bytes 25165824 | tf_op jit(solution)/shard_map/conv_general_dilated | solution.py:41
  187.9 31.9 %copy.49 = bf16[4,192,4096]{1,0,2:T(4,128)(2,1)S(1)} copy(bf16[4,192,4096]{1,2,0:T(8,128)(2,1)S(1)} %fusion.7) | data formatting | bytes 12582912 | tf_op jit(solution)/shard_map/convert_element_type | solution.py:66
  219.8 190.2 %all_to_all.4 = bf16[4,192,4096]{1,0,2:T(4,128)(2,1)} all-to-all(bf16[4,192,4096]{1,0,2:T(4,128)(2,1)S(1)} %copy.49), channel_id=1, replica_groups=mesh['group'=2,'swap'=8,'image'=2] {'swap'}, dimensions={2} | all-to-all | bytes 12582912 | tf_op jit(solution)/shard_map/all_to_all | solution.py:67
  410.0 13.5 %copy.50 = bf16[4,192,4096]{2,1,0:T(8,128)(2,1)} copy(bf16[4,192,4096]{1,0,2:T(4,128)(2,1)} %all_to_all.4) | data formatting | bytes 12582912 | tf_op jit(solution)/shard_map/all_to_all | solution.py:67
  423.6 9.1 %copy.55 = f32[96,8,8,512]{3,2,1,0:T(8,128)S(1)} copy(bf16[96,8,8,512]{3,1,2,0:T(8,128)(2,1)} %bitcast.77) | data formatting | bytes 18874368
  438.7 10.6 %bitcast_bitcast_fusion = f32[4,8,192,512]{3,1,2,0:T(8,128)} fusion(f32[4,192,8,512]{3,2,1,0:T(8,128)} %bitcast.71), kind=kLoop, calls=%fused_computation.16 | loop fusion | bytes 25165824 | tf_op jit(solution)/shard_map/convert_element_type | solution.py:67
  449.4 16.7 %copy.51 = f32[4,8,192,512]{3,2,1,0:T(8,128)} copy(f32[4,8,192,512]{3,1,2,0:T(8,128)} %bitcast_bitcast_fusion) | data formatting | bytes 25165824 | tf_op jit(solution)/shard_map/convert_element_type | solution.py:67
  466.1 9.0 %fusion.15 = bf16[4,1536,512]{2,1,0:T(8,128)(2,1)} fusion(f32[4,8,192,512]{3,2,1,0:T(8,128)} %copy.51, f32[1536]{0:T(1024)S(1)} %copy-done.6, f32[1536]{0:T(1024)S(1)} %copy-done.7, f32[4,512]{1,0:T(4,128)S(1)} %add_rsqrt_fusion, f32[4,512]{1,0:T(4,128)S(1)} %broadcast_multiply_fusion), kind=kLoop, calls=%fused_computation.21 | loop fusion | flops 15728640 | bytes 18903040 | tf_op jit(solution)/shard_map/convert_element_type | solution.py:77
  475.1 8.7 %copy.52 = bf16[4,512,1536]{2,1,0:T(8,128)(2,1)} copy(bf16[4,512,1536]{1,2,0:T(8,128)(2,1)} %bitcast.78) | data formatting | bytes 12582912 | tf_op jit(solution)/shard_map/convert_element_type | solution.py:77
  486.4 21.3 %all-gather.3.cloned.1.call-done = bf16[4096,1536]{1,0:T(8,128)(2,1)} async-done(((bf16[2048,1536]{1,0:T(8,128)(2,1)}), bf16[4096,1536]{1,0:T(8,128)(2,1)}) %all-gather.3.cloned.1.call-update) | async-done | bytes 12582928 | tf_op jit(solution)/shard_map/all_gather | solution.py:79
  507.7 8.3 convolution_convert_fusion
  516.0 20.1 %fusion.20 = f32[4096,3072]{1,0:T(8,128)} fusion(bf16[4096,32]{0,1:T(8,128)(2,1)S(1)} %convolution_convert_fusion, bf16[32,3072]{1,0:T(8,128)(2,1)S(1)} %copy-done), kind=kOutput, calls=%fused_computation.33 | convolution fusion | flops 805306368 | bytes 50790400 | tf_op jit(solution)/shard_map/dot_general | solution.py:86
  536.2 112.2 %all-gather.5.cloned.1.call-done = bf16[1536,3072]{1,0:T(8,128)(2,1)} async-done(((bf16[192,3072]{1,0:T(8,128)(2,1)}), bf16[1536,3072]{1,0:T(8,128)(2,1)}) %all-gather.5.cloned.1.call-update) | async-done | bytes 9437200 | tf_op jit(solution)/shard_map/all_gather | solution.py:82
  648.3 64.7 %fusion.5 = bf16[4096,3072]{1,0:T(8,128)(2,1)} fusion(bf16[4096,3072]{1,0:T(8,128)(2,1)} %bitcast.80, f32[4096,3072]{1,0:T(8,128)} %fusion.20, bf16[4096,1536]{1,0:T(8,128)(2,1)} %all-gather.3.cloned.1.call-done, bf16[1536,3072]{1,0:T(8,128)(2,1)} %all-gather.5.cloned.1.call-done), kind=kOutput, calls=%fused_computation.6 | convolution fusion | flops 38818283520 | bytes 122683392 | tf_op jit(solution)/shard_map/dot_general | solution.py:84
  713.0 12.9 %fusion.21 = f32[4096,32]{0,1:T(8,128)} fusion(bf16[4096,3072]{1,0:T(8,128)(2,1)} %fusion.5, bf16[32,3072]{1,0:T(8,128)(2,1)S(1)} %copy-done), kind=kOutput, calls=%fused_computation.34 | convolution fusion | flops 805306368 | bytes 25886720 | tf_op jit(solution)/shard_map/dot_general | solution.py:92
  726.0 11.7 %convolution_multiply_fusion = f32[32,3072]{1,0:T(8,128)} fusion(bf16[4096,32]{0,1:T(8,128)(2,1)S(1)} %convolution_convert_fusion, bf16[4096,3072]{1,0:T(8,128)(2,1)} %fusion.5), kind=kOutput, calls=%fused_computation.25 | convolution fusion | flops 805404672 | bytes 25821184 | tf_op jit(solution)/shard_map/dot_general | solution.py:91
  737.7 5.2 all-reduce.4.cloned.1.call-done
  742.8 9.8 %convolution_multiply_fusion.1 = f32[1536,32]{0,1:T(8,128)} fusion(bf16[4096,1536]{1,0:T(8,128)(2,1)} %all-gather.3.cloned.1.call-done, f32[4096,32]{0,1:T(8,128)} %all-reduce.4.cloned.1.call-done), kind=kOutput, calls=%fused_computation.28 | convolution fusion | flops 2415968256 | bytes 13303808 | tf_op jit(solution)/shard_map/dot_general | solution.py:96
  752.7 74.7 %all-reduce.6.cloned.1.call-done = (f32[1536,32]{0,1:T(8,128)}, f32[32,3072]{1,0:T(8,128)}) async-done(((f32[1536,32]{0,1:T(8,128)}, f32[32,3072]{1,0:T(8,128)}), (f32[1536,32]{0,1:T(8,128)}, f32[32,3072]{1,0:T(8,128)})) %all-reduce.6.cloned.1.call-update) | async-done | bytes 589840 | tf_op jit(solution)/shard_map/psum | solution.py:103
  (43 shorter events, 27.1 us)
Async XLA Ops:
  7.2 508.9 %copy-start = (bf16[32,3072]{1,0:T(8,128)(2,1)S(1)}, bf16[32,3072]{1,0:T(8,128)(2,1)}, u32[]{:S(2)}) copy-start(bf16[32,3072]{1,0:T(8,128)(2,1)} %param.18) | copy-start | bytes 589828
  7.2 500.5 %all-gather.3.cloned.1.call-start = ((), (), s32[]{:S(2)}) async-start(), calls=%async_computation.1 | async-start | bytes 18874368 | tf_op jit(solution)/shard_map/all_gather | solution.py:79
  40.2 5.3 copy-start.2
  45.5 4.2 copy-start.9
  167.4 17.9 %copy-start.8 = (f32[192]{0:T(256)S(1)}, f32[192]{0:T(256)}, u32[]{:S(2)}) copy-start(f32[192]{0:T(256)} %param.12) | copy-start | bytes 2308
  432.6 4.5 copy-start.1
  449.4 16.8 %copy-start.6 = (f32[1536]{0:T(1024)S(1)}, f32[1536]{0:T(1024)}, u32[]{:S(2)}) copy-start(f32[1536]{0:T(1024)} %param.14) | copy-start | bytes 18436
  449.4 16.8 %copy-start.7 = (f32[1536]{0:T(1024)S(1)}, f32[1536]{0:T(1024)}, u32[]{:S(2)}) copy-start(f32[1536]{0:T(1024)} %param.13) | copy-start | bytes 18436
  466.1 17.8 %copy-start.5 = (s32[192,24]{0,1:T(8,128)S(1)}, s32[192,24]{0,1:T(8,128)}, u32[]{:S(2)}) copy-start(s32[192,24]{0,1:T(8,128)} %param.16) | copy-start | bytes 55300
  466.1 18.6 %copy-start.3 = (bf16[192,3072]{1,0:T(8,128)(2,1)S(1)}, bf16[192,3072]{1,0:T(8,128)(2,1)}, u32[]{:S(2)}) copy-start(bf16[192,3072]{1,0:T(8,128)(2,1)} %param.15) | copy-start | bytes 3538948
  475.1 32.6 %copy-start.4 = (bf16[1536,32]{0,1:T(8,128)(2,1)S(1)}, bf16[1536,32]{0,1:T(8,128)(2,1)}, u32[]{:S(2)}) copy-start(bf16[1536,32]{0,1:T(8,128)(2,1)} %param.17) | copy-start | bytes 294916
  483.8 164.5 %all-gather.5.cloned.1.call-start = ((), (), s32[]{:S(2)}) async-start(), calls=%async_computation.2 | async-start | bytes 10616832 | tf_op jit(solution)/shard_map/all_gather | solution.py:82
  486.4 256.5 %all-reduce.4.cloned.1.call-start = ((), (), s32[]{:S(2)}) async-start(), calls=%async_computation.3 | async-start | bytes 1048576 | tf_op jit(solution)/shard_map/psum | solution.py:95
  725.9 101.4 %all-reduce.6.cloned.1.call-start = ((), (), s32[]{:S(2)}) async-start(), calls=%async_computation.4 | async-start | bytes 1179648 | tf_op jit(solution)/shard_map/psum | solution.py:103
Sparse Core Ops, SparseCore 0:
  484.0 23.7 all-gather.2
  509.9 138.3 all-gather.4
  726.0 16.7 all-reduce.3
  752.8 74.5 all-reduce.5
where the time goes:
time: 845 us; the launch traced here: 837 us
  matrix products  223 us (26%)
  waiting for transfers between devices  213 us (25%)
  blocking collectives  190 us (22%)
  local copies, waits for them, and re-layouts  176 us (21%)
  other arithmetic  20 us (2%)
  between operations  14.2 us (2%)
    all_to_all x1, blocking collectives, shards(): lax.all_to_all(conv, 'swap', split_axis=2, concat_axis=1, tiled=True)  190 us
    all_gather x1, waiting for transfers between devices, shards(): shard_rows = lax.all_gather(local_weight, 'swap', axis=0, tiled=True)  112 us
    conv_general_dilated x1, matrix products, depthwise(): lax.conv_general_dilated(maps, taps, (1, 1), ((half_span, half_span), (ha...  95.5 us
    psum x1, waiting for transfers between devices, shards(): grad_a, grad_b = lax.psum((grad_a_local, grad_b_local), 'swap')  74.7 us
    dot_general x1, matrix products, shards(): jnp.dot(columns, shard_rows, preferred_element_type=jnp.float32)  64.7 us
    conv_general_dilated x4, local copies, waits for them, and re-layouts, depthwise(): lax.conv_general_dilated(maps, taps, (1, 1), ((half_span, half_span), (ha...  43.4 us
    unnamed x25, local copies, waits for them, and re-layouts  40 us
    convert_element_type x1, local copies, waits for them, and re-layouts, shards(): conv = depthwise(images_in, kernel, conv_bias, W).astype(jnp.bfloat16)  31.9 us
  transfers between devices with their start and end apart: 4, of which 4 were waited for; matrix products, arithmetic and copies ran while one was open for 5% of the time, Pallas kernels for 0%

commit v1 on v0

--- a/solution.py
+++ b/solution.py
@@ -64,9 +64,10 @@
     cotangent,
 ):
     conv = depthwise(images_in, kernel, conv_bias, W).astype(jnp.bfloat16)
-    values = lax.all_to_all(conv, "swap", split_axis=2, concat_axis=1, tiled=True).astype(
-        jnp.float32
-    )
+    values = jnp.concatenate(
+        lax.all_to_all(jnp.stack(jnp.split(conv, lax.axis_size("swap"), axis=2)), "swap", 0, 0),
+        axis=1,
+    ).astype(jnp.float32)
     average = jnp.mean(values, axis=1, keepdims=True)
     centred = values - average
     variance = jnp.mean(centred * centred, axis=1, keepdims=True)

time: 845 us -> 731 us (0.87)
  local copies, waits for them, and re-layouts: 176 us -> 111 us
  blocking collectives: 190 us -> 146 us
    convert_element_type x3 -> x0, local copies, waits for them, and re-layouts: 59.2 us -> none  [the longest x1 31.9 us: shards(): conv = depthwise(images_in, kernel, conv_bias, W).astype(jnp.bfloat16)]
    all_to_all x1, blocking collectives: 190 us -> 146 us  [shards(): lax.all_to_all(jnp.stack(jnp.split(conv, lax.axis_size('swap'), axis=2)),...]
    all_to_all x1 -> x0, local copies, waits for them, and re-layouts: 13.5 us -> none  [shards(): lax.all_to_all(conv, 'swap', split_axis=2, concat_axis=1, tiled=True)]
    another operation x0 -> x2, local copies, waits for them, and re-layouts: none -> 12.2 us  [shards(): jnp.stack(jnp.split(conv, lax.axis_size('swap'), axis=2))]
    unnamed x25 -> x29, local copies, waits for them, and re-layouts: 40 us -> 34.9 us
  transfers between devices with their start and end apart: 4 -> 4, of which waited for: 4 -> 4; matrix products, arithmetic and copies ran while one was open for 5% -> 6% of each run, Pallas kernels for 0% -> 0%
where the time goes in v1:
time: 731 us; the launch traced here: 723 us
  matrix products  223 us (31%)
  waiting for transfers between devices  213 us (29%)
  blocking collectives  146 us (20%)
  local copies, waits for them, and re-layouts  111 us (15%)
  other arithmetic  15.4 us (2%)
  between operations  14.2 us (2%)
    all_to_all x1, blocking collectives, shards(): lax.all_to_all(jnp.stack(jnp.split(conv, lax.axis_size('swap'), axis=2)),...  146 us
    all_gather x1, waiting for transfers between devices, shards(): shard_rows = lax.all_gather(local_weight, 'swap', axis=0, tiled=True)  112 us
    conv_general_dilated x1, matrix products, depthwise(): lax.conv_general_dilated(maps, taps, (1, 1), ((half_span, half_span), (ha...  95.7 us
    psum x1, waiting for transfers between devices, shards(): grad_a, grad_b = lax.psum((grad_a_local, grad_b_local), 'swap')  74.7 us
    dot_general x1, matrix products, shards(): jnp.dot(columns, shard_rows, preferred_element_type=jnp.float32)  64.7 us
    conv_general_dilated x4, local copies, waits for them, and re-layouts, depthwise(): lax.conv_general_dilated(maps, taps, (1, 1), ((half_span, half_span), (ha...  43.4 us
    unnamed x29, local copies, waits for them, and re-layouts  34.9 us
    all_gather x1, waiting for transfers between devices, shards(): tokens = lax.all_gather(own_rows, 'image', axis=0, tiled=True)  21.3 us
  transfers between devices with their start and end apart: 4, of which 4 were waited for; matrix products, arithmetic and copies ran while one was open for 6% of the time, Pallas kernels for 0%

profile of v1, /device:TPU:0, one launch (start us, length us, event | category | flops | bytes accessed | tf_op | source)
XLA Modules:
  0.0 723.2 jit_solution(9437239590115696736)
XLA Ops:
  8.1 10.6 %copy.23 = bf16[4,192,4096]{1,2,0:T(8,128)(2,1)} copy(bf16[4,192,4096]{2,1,0:T(8,128)(2,1)} %param.10) | data formatting | bytes 12582912 | tf_op args[0]
  18.7 11.5 %copy.33 = bf16[192,64,4,64]{0,1,3,2:T(8,128)(2,1)} copy(bf16[192,64,4,64]{0,3,1,2:T(8,128)(2,1)} %bitcast.93) | data formatting | bytes 12582912
  30.2 10.0 %pad.clone = bf16[192,64,4,72]{0,1,3,2:T(8,128)(2,1)} pad(bf16[192,64,4,64]{0,1,3,2:T(8,128)(2,1)} %copy.33, bf16[]{:T(256)} %constant.37), padding=0_0x0_0x0_0x3_5 | pad | bytes 13369346 | tf_op jit(solution)/shard_map/reshape | solution.py:38
  40.2 3.4 slice.2
  45.5 4.2 fusion.8
  49.7 95.7 %broadcast_select_fusion = f32[64,32,9,192]{3,1,2,0:T(8,128)S(1)} fusion(pred[32,9]{0,1:T(8,128)(4,1)S(1)} %copy-done.8, bf16[192,1,7,7]{0,1,3,2:T(2,128)(2,1)S(1)} %reshape.58, bf16[192,64,4,8,15]{0,1,4,3,2:T(8,128)(2,1)S(1)} %fusion.8), kind=kOutput, calls=%fused_computation.25 | convolution fusion | flops 341065728 | bytes 25971360 | tf_op jit(solution)/shard_map/conv_general_dilated | solution.py:41
  145.4 20.1 %copy.27 = f32[64,32,9,192]{3,0,2,1:T(8,128)S(1)} copy(f32[64,32,9,192]{3,1,2,0:T(8,128)S(1)} %broadcast_select_fusion) | data formatting | bytes 28311552 | tf_op jit(solution)/shard_map/conv_general_dilated | solution.py:41
  165.5 2.0 slice_bitcast_fusion
  167.5 17.9 %copy.28 = f32[4,192,64,64]{1,3,2,0:T(8,128)S(1)} copy(f32[4,192,64,64]{1,2,3,0:T(8,128)S(1)} %slice_bitcast_fusion) | data formatting | bytes 25165824 | tf_op jit(solution)/shard_map/conv_general_dilated | solution.py:41
  185.4 2.5 fusion.7
  196.5 11.1 %copy.29 = bf16[8,4,192,512]{3,2,1,0:T(8,128)(2,1)} copy(bf16[8,4,192,512]{2,3,1,0:T(8,128)(2,1)} %fusion.21) | data formatting | bytes 12582912 | tf_op jit(solution)/shard_map/stack | solution.py:68
  207.6 146.0 %all_to_all.5 = bf16[8,4,192,512]{3,2,1,0:T(8,128)(2,1)S(1)} all-to-all(bf16[8,4,192,512]{3,2,1,0:T(8,128)(2,1)} %copy.29), channel_id=1, replica_groups=mesh['group'=2,'swap'=8,'image'=2] {'swap'}, dimensions={0} | all-to-all | bytes 12582912 | tf_op jit(solution)/shard_map/all_to_all | solution.py:68
  356.2 4.4 fusion.15
  360.6 8.7 %copy.31 = bf16[4,512,1536]{2,1,0:T(8,128)(2,1)} copy(bf16[4,512,1536]{1,2,0:T(8,128)(2,1)} %bitcast.95) | data formatting | bytes 12582912 | tf_op jit(solution)/shard_map/convert_element_type | solution.py:78
  372.0 21.3 %all-gather.3.cloned.1.call-done = bf16[4096,1536]{1,0:T(8,128)(2,1)} async-done(((bf16[2048,1536]{1,0:T(8,128)(2,1)}), bf16[4096,1536]{1,0:T(8,128)(2,1)}) %all-gather.3.cloned.1.call-update) | async-done | bytes 12582928 | tf_op jit(solution)/shard_map/all_gather | solution.py:80
  393.3 8.3 %convolution_convert_fusion = bf16[4096,32]{0,1:T(8,128)(2,1)S(1)} fusion(bf16[4096,1536]{1,0:T(8,128)(2,1)} %all-gather.3.cloned.1.call-done, bf16[1536,32]{0,1:T(8,128)(2,1)S(1)} %copy-done.3), kind=kOutput, calls=%fused_computation.26 | convolution fusion | flops 402784256 | bytes 12943360 | tf_op jit(solution)/shard_map/dot_general | solution.py:86
  401.6 20.1 %fusion.29 = f32[4096,3072]{1,0:T(8,128)} fusion(bf16[4096,32]{0,1:T(8,128)(2,1)S(1)} %convolution_convert_fusion, bf16[32,3072]{1,0:T(8,128)(2,1)S(1)} %copy-done), kind=kOutput, calls=%fused_computation.50 | convolution fusion | flops 805306368 | bytes 50790400 | tf_op jit(solution)/shard_map/dot_general | solution.py:87
  421.7 112.2 %all-gather.5.cloned.1.call-done = bf16[1536,3072]{1,0:T(8,128)(2,1)} async-done(((bf16[192,3072]{1,0:T(8,128)(2,1)}), bf16[1536,3072]{1,0:T(8,128)(2,1)}) %all-gather.5.cloned.1.call-update) | async-done | bytes 9437200 | tf_op jit(solution)/shard_map/all_gather | solution.py:83
  533.9 64.7 %fusion.5 = bf16[4096,3072]{1,0:T(8,128)(2,1)} fusion(bf16[4096,3072]{1,0:T(8,128)(2,1)} %bitcast.97, f32[4096,3072]{1,0:T(8,128)} %fusion.29, bf16[4096,1536]{1,0:T(8,128)(2,1)} %all-gather.3.cloned.1.call-done, bf16[1536,3072]{1,0:T(8,128)(2,1)} %all-gather.5.cloned.1.call-done), kind=kOutput, calls=%fused_computation.6 | convolution fusion | flops 38818283520 | bytes 122683392 | tf_op jit(solution)/shard_map/dot_general | solution.py:85
  598.6 13.0 %fusion.30 = f32[4096,32]{0,1:T(8,128)} fusion(bf16[4096,3072]{1,0:T(8,128)(2,1)} %fusion.5, bf16[32,3072]{1,0:T(8,128)(2,1)S(1)} %copy-done), kind=kOutput, calls=%fused_computation.51 | convolution fusion | flops 805306368 | bytes 25886720 | tf_op jit(solution)/shard_map/dot_general | solution.py:93
  611.7 11.7 %convolution_multiply_fusion = f32[32,3072]{1,0:T(8,128)} fusion(bf16[4096,32]{0,1:T(8,128)(2,1)S(1)} %convolution_convert_fusion, bf16[4096,3072]{1,0:T(8,128)(2,1)} %fusion.5), kind=kOutput, calls=%fused_computation.27 | convolution fusion | flops 805404672 | bytes 25821184 | tf_op jit(solution)/shard_map/dot_general | solution.py:92
  623.4 5.2 all-reduce.4.cloned.1.call-done
  628.6 9.7 %convolution_multiply_fusion.1 = f32[1536,32]{0,1:T(8,128)} fusion(bf16[4096,1536]{1,0:T(8,128)(2,1)} %all-gather.3.cloned.1.call-done, f32[4096,32]{0,1:T(8,128)} %all-reduce.4.cloned.1.call-done), kind=kOutput, calls=%fused_computation.30 | convolution fusion | flops 2415968256 | bytes 13303808 | tf_op jit(solution)/shard_map/dot_general | solution.py:97
  638.4 74.7 %all-reduce.6.cloned.1.call-done = (f32[1536,32]{0,1:T(8,128)}, f32[32,3072]{1,0:T(8,128)}) async-done(((f32[1536,32]{0,1:T(8,128)}, f32[32,3072]{1,0:T(8,128)}), (f32[1536,32]{0,1:T(8,128)}, f32[32,3072]{1,0:T(8,128)})) %all-reduce.6.cloned.1.call-update) | async-done | bytes 589840 | tf_op jit(solution)/shard_map/psum | solution.py:104
  (45 shorter events, 19.8 us)
Async XLA Ops:
  7.2 394.4 %copy-start = (bf16[32,3072]{1,0:T(8,128)(2,1)S(1)}, bf16[32,3072]{1,0:T(8,128)(2,1)}, u32[]{:S(2)}) copy-start(bf16[32,3072]{1,0:T(8,128)(2,1)} %param.18) | copy-start | bytes 589828
  7.2 386.1 %all-gather.3.cloned.1.call-start = ((), (), s32[]{:S(2)}) async-start(), calls=%async_computation.1 | async-start | bytes 18874368 | tf_op jit(solution)/shard_map/all_gather | solution.py:80
  40.2 5.3 copy-start.1
  45.5 4.2 copy-start.8
  167.5 17.9 %copy-start.7 = (f32[192]{0:T(256)S(1)}, f32[192]{0:T(256)}, u32[]{:S(2)}) copy-start(f32[192]{0:T(256)} %param.12) | copy-start | bytes 2308
  207.6 148.6 %copy-start.5 = (f32[1536]{0:T(1024)S(1)}, f32[1536]{0:T(1024)}, u32[]{:S(2)}) copy-start(f32[1536]{0:T(1024)} %param.14) | copy-start | bytes 18436
  207.6 148.6 %copy-start.6 = (f32[1536]{0:T(1024)S(1)}, f32[1536]{0:T(1024)}, u32[]{:S(2)}) copy-start(f32[1536]{0:T(1024)} %param.13) | copy-start | bytes 18436
  360.6 8.8 %copy-start.4 = (s32[192,24]{0,1:T(8,128)S(1)}, s32[192,24]{0,1:T(8,128)}, u32[]{:S(2)}) copy-start(s32[192,24]{0,1:T(8,128)} %param.16) | copy-start | bytes 55300
  360.6 9.7 %copy-start.2 = (bf16[192,3072]{1,0:T(8,128)(2,1)S(1)}, bf16[192,3072]{1,0:T(8,128)(2,1)}, u32[]{:S(2)}) copy-start(bf16[192,3072]{1,0:T(8,128)(2,1)} %param.15) | copy-start | bytes 3538948
  360.6 32.7 %copy-start.3 = (bf16[1536,32]{0,1:T(8,128)(2,1)S(1)}, bf16[1536,32]{0,1:T(8,128)(2,1)}, u32[]{:S(2)}) copy-start(bf16[1536,32]{0,1:T(8,128)(2,1)} %param.17) | copy-start | bytes 294916
  369.4 164.5 %all-gather.5.cloned.1.call-start = ((), (), s32[]{:S(2)}) async-start(), calls=%async_computation.2 | async-start | bytes 10616832 | tf_op jit(solution)/shard_map/all_gather | solution.py:83
  371.9 256.7 %all-reduce.4.cloned.1.call-start = ((), (), s32[]{:S(2)}) async-start(), calls=%async_computation.3 | async-start | bytes 1048576 | tf_op jit(solution)/shard_map/psum | solution.py:96
  611.7 101.4 %all-reduce.6.cloned.1.call-start = ((), (), s32[]{:S(2)}) async-start(), calls=%async_computation.4 | async-start | bytes 1179648 | tf_op jit(solution)/shard_map/psum | solution.py:104
Sparse Core Ops, SparseCore 0:
  369.5 23.7 all-gather.2
  395.5 138.3 all-gather.4
  611.8 16.7 all-reduce.3
  638.5 74.4 all-reduce.5
